TPU v7x, 512 devices: a whole 4x8x8 slice. The times are simulated.
512 devices in a mesh: section: 16 (over x_lo, z), dp: 32 (over x_hi, y, core).
Axes of the slice: x: 4 (x_hi: 2, x_lo: 2; x = x_hi * 2 + x_lo), y: 8, z: 8, core: 2. Of those that a mesh axis runs over, the one named last changes fastest.
Arguments:
- acts_down: bfloat16 [3, 16, 32, 16, 16, 256], P(None, 'section', 'dp'), may hold values from -6 to 6
- acts_up: bfloat16 [3, 16, 32, 16, 16, 256], P(None, 'section', 'dp'), may hold values from -6 to 6
- front_down: bfloat16 [16, 32, 16, 16, 256], P('section', 'dp'), may hold values from -6 to 6
- front_up: bfloat16 [16, 32, 16, 16, 256], P('section', 'dp'), may hold values from -6 to 6
- master: float32 [16, 2304, 256], P('section', 'dp'), may hold values from -4 to 4
- moment_first: float32 [16, 2304, 256], P('section', 'dp'), may hold values from -36 to 36
- moment_second: float32 [16, 2304, 256], P('section', 'dp'), may hold values from 10 to 100
Outputs:
- dx_down: bfloat16 [3, 16, 32, 16, 16, 256], P(None, 'section', 'dp')
- dx_up: bfloat16 [3, 16, 32, 16, 16, 256], P(None, 'section', 'dp')
- new_weight: bfloat16 [16, 2304, 256], P('section', 'dp')
- new_master: float32 [16, 2304, 256], P('section', 'dp')
- new_first: float32 [16, 2304, 256], P('section', 'dp')
- new_second: float32 [16, 2304, 256], P('section', 'dp')
All inputs are finite; a program needn't handle non-finite values.
Results may differ from a plain program's by a relative error of at most 0.0025.
The roundings to bfloat16 on the way count: a program that leaves them out, or rounds other values in their place, can miss the bound.
Values may be sent and summed in bfloat16 or wider, within the bound.
No kernel may reach another device: no remote copies, remote signals or barrier semaphores. Data moves between devices by JAX's collectives and lax.ppermute only.
A program may use at most 64 MiB of HBM per device.

v0:
```python
import jax
import jax.numpy as jnp
from jax import lax
from jax.sharding import PartitionSpec as P

TICKS = 3
beta_first = 0.9
beta_second = 0.95
learn_rate = 0.01
decay_rate = 0.1
epsilon = 1e-08


def from_partner(value, axis, stride):
    return lax.ppermute(value, axis, [(i, i ^ 1 << stride) for i in range(lax.axis_size(axis))])


def passed_along(value, axis, by):
    length = lax.axis_size(axis)
    pairs = [(i, i + by) for i in range(length) if 0 <= i + by < length]
    return lax.ppermute(value, axis, pairs)


def shifted_taps(feature, direction):
    images, height, columns, channels = feature.shape
    padded = jnp.pad(feature, ((0, 0), (1, 1), (1, 1), (0, 0)))
    pieces = []
    for row_step in range(3):
        for col_step in range(3):
            row_start = 1 + direction * (row_step - 1)
            col_start = 1 + direction * (col_step - 1)
            pieces.append(
                padded[:, row_start : row_start + height, col_start : col_start + columns, :]
            )
    return jnp.concatenate(pieces, axis=3).reshape(images * height * columns, 9 * channels)


def section_front(inputs, incoming, weight):
    channels = inputs.shape[-1]
    factor = (9 * channels) ** (-0.5)
    taps_front = shifted_taps(incoming, -1).reshape(-1, 9, channels)
    kernel = weight.reshape(9, channels, channels)
    grad_hidden = lax.dot_general(
        taps_front, kernel, (((1, 2), (0, 2)), ((), ())), preferred_element_type=jnp.float32
    )
    grad_hidden = factor * grad_hidden.reshape(inputs.shape)
    widened = inputs.astype(jnp.float32)
    hidden, pullback = jax.vjp(jax.nn.gelu, widened)
    outgoing = (incoming.astype(jnp.float32) + pullback(grad_hidden)[0]).astype(jnp.bfloat16)
    return (outgoing, hidden.astype(jnp.bfloat16))


def weight_term(hiddens, seen):
    channels = hiddens[0].shape[-1]
    factor = (9 * channels) ** (-0.5)
    summed = jnp.zeros((9 * channels, channels), jnp.float32)
    for hidden, incoming in zip(hiddens, seen):
        taps_hidden = shifted_taps(hidden, 1)
        summed = summed + lax.dot_general(
            taps_hidden,
            incoming.reshape(-1, channels),
            (((0,), (0,)), ((), ())),
            preferred_element_type=jnp.float32,
        )
    return factor * summed


def per_device(acts_down, acts_up, front_down, front_up, master, moment_first, moment_second):
    sections = lax.axis_size("section")
    own_rows = master[0].astype(jnp.bfloat16)
    mirror_rows = own_rows
    for bit_number in range(sections.bit_length() - 1):
        mirror_rows = from_partner(mirror_rows, "section", bit_number)
    own_weight, mirror_weight = (
        lax.all_gather(own_rows, "dp", axis=0, tiled=True),
        lax.all_gather(mirror_rows, "dp", axis=0, tiled=True),
    )
    grad_down = front_down[0]
    grad_up = front_up[0]
    seen_down = []
    seen_up = []
    hidden_down = []
    hidden_up = []
    outs_down = []
    outs_up = []
    for tick_index in range(TICKS):
        seen_down.append(grad_down)
        seen_up.append(grad_up)
        next_down, hid_down = section_front(acts_down[tick_index, 0], grad_down, own_weight)
        next_up, hid_up = section_front(acts_up[tick_index, 0], grad_up, mirror_weight)
        hidden_down.append(hid_down)
        hidden_up.append(hid_up)
        outs_down.append(next_down)
        outs_up.append(next_up)
        if tick_index + 1 < TICKS:
            grad_down = passed_along(next_down, "section", -1)
            grad_up = passed_along(next_up, "section", 1)
    term_down = weight_term(hidden_down, seen_down)
    term_up = weight_term(hidden_up, seen_up)
    full_down, full_up = (
        lax.psum(term_down.astype(jnp.bfloat16), "dp").astype(jnp.float32),
        lax.psum(term_up.astype(jnp.bfloat16), "dp").astype(jnp.float32),
    )
    shard_rows = term_down.shape[0] // lax.axis_size("dp")
    row_start = lax.axis_index("dp") * shard_rows
    down_rows = lax.dynamic_slice_in_dim(full_down, row_start, shard_rows, 0)
    up_rows = lax.dynamic_slice_in_dim(full_up, row_start, shard_rows, 0)
    mirror_grad = up_rows
    for bit_number in range(sections.bit_length() - 1):
        mirror_grad = from_partner(mirror_grad.astype(jnp.bfloat16), "section", bit_number).astype(
            mirror_grad.dtype
        )
    gradient = down_rows + mirror_grad
    old_master = master[0]
    new_first = beta_first * moment_first[0] + (1.0 - beta_first) * gradient
    new_second = beta_second * moment_second[0] + (1.0 - beta_second) * gradient * gradient
    new_master = old_master - learn_rate * (
        new_first / (jnp.sqrt(new_second) + epsilon) + decay_rate * old_master
    )
    return (
        jnp.stack(outs_down)[:, None],
        jnp.stack(outs_up)[:, None],
        new_master.astype(jnp.bfloat16)[None],
        new_master[None],
        new_first[None],
        new_second[None],
    )


def solution(mesh):
    placed = (
        P(None, "section", "dp", None, None, None),
        P(None, "section", "dp", None, None, None),
        P("section", "dp", None, None, None),
        P("section", "dp", None, None, None),
        P("section", "dp", None),
        P("section", "dp", None),
        P("section", "dp", None),
    )
    return jax.shard_map(
        per_device,
        mesh=mesh,
        in_specs=placed,
        out_specs=(
            P(None, "section", "dp", None, None, None),
            P(None, "section", "dp", None, None, None),
            P("section", "dp", None),
            P("section", "dp", None),
            P("section", "dp", None),
            P("section", "dp", None),
        ),
        check_vma=False,
    )
```

profile of v0, /device:TPU:2, one launch (start us, length us, event | category | flops | bytes accessed | tf_op | source)
XLA Modules:
  0.0 534.1 jit_solution(15789119350843120180)
XLA Ops:
  8.8 4.3 collective-permute-start.2
  32.8 6.1 %collective-permute-start.3 = (bf16[72,256]{1,0:T(8,128)(2,1)S(1)}, bf16[72,256]{1,0:T(8,128)(2,1)S(1)}, u32[]{:S(2)}, u32[]{:S(2)}) collective-permute-start(bf16[72,256]{1,0:T(8,128)(2,1)S(1)} %collective-permute-done.2), channel_id=1, source_target_pairs={{0,64},{32,96},{64,0},{96,32},{128,192},{160,224},{192,128},{224,1... | collective-permute-start | bytes 110600 | tf_op jit(solution)/shard_map/ppermute | solution.py:15
  40.8 9.1 %collective-permute-start.4 = (bf16[72,256]{1,0:T(8,128)(2,1)S(1)}, bf16[72,256]{1,0:T(8,128)(2,1)S(1)}, u32[]{:S(2)}, u32[]{:S(2)}) collective-permute-start(bf16[72,256]{1,0:T(8,128)(2,1)S(1)} %collective-permute-done.3), channel_id=1, source_target_pairs={{0,128},{32,160},{64,192},{96,224},{128,0},{160,32},{192,64},{224,... | collective-permute-start | bytes 110600 | tf_op jit(solution)/shard_map/ppermute | solution.py:15
  55.4 3.5 dot_general.48
  60.3 3.3 fusion.219
  63.5 35.4 %all-gather.3.cloned.1.call-done = bf16[2304,256]{1,0:T(8,128)(2,1)} async-done(((bf16[72,256]{1,0:T(8,128)(2,1)}), bf16[2304,256]{1,0:T(8,128)(2,1)}) %all-gather.3.cloned.1.call-update) | async-done | bytes 1179664 | tf_op jit(solution)/shard_map/all_gather | solution.py:75
  98.9 2.9 fusion.119
  101.8 6.8 %collective-permute-start = (bf16[1,16,16,256]{3,2,1,0:T(8,128)(2,1)S(1)}, bf16[1,16,16,256]{3,2,1,0:T(8,128)(2,1)S(1)}, u32[]{:S(2)}, u32[]{:S(2)}) collective-permute-start(bf16[1,16,16,256]{3,2,1,0:T(8,128)(2,1)S(1)} %bitcast.548), channel_id=1, source_target_pairs={{32,0},{64,32},{96,64},{128,96},{160,128},{192,160},{224,192},{256... | collective-permute-start | bytes 393224 | tf_op jit(solution)/shard_map/ppermute | solution.py:21
  109.2 3.6 dot_general.54
  119.9 3.5 dot_general.50
  123.4 3.5 fusion.125
  126.9 4.6 collective-permute-start.1
  131.6 51.5 %all-gather.5.cloned.1.call-done = bf16[2304,256]{1,0:T(8,128)(2,1)} async-done(((bf16[72,256]{1,0:T(8,128)(2,1)}), bf16[2304,256]{1,0:T(8,128)(2,1)}) %all-gather.5.cloned.1.call-update) | async-done | bytes 1179664 | tf_op jit(solution)/shard_map/all_gather | solution.py:76
  183.1 3.0 fusion.139
  186.1 3.7 collective-permute-start.6
  191.8 4.9 collective-permute-done.6
  203.0 3.5 dot_general.56
  206.5 3.0 fusion.145
  211.7 3.7 fusion.7
  215.3 3.4 collective-permute-done.7
  238.7 256.8 %all-reduce.15.cloned.1.call-done = (bf16[2304,256]{1,0:T(8,128)(2,1)}, bf16[2304,256]{1,0:T(8,128)(2,1)}) async-done(((bf16[2304,256]{1,0:T(8,128)(2,1)}, bf16[2304,256]{1,0:T(8,128)(2,1)}), (bf16[2304,256]{1,0:T(8,128)(2,1)}, bf16[2304,256]{1,0:T(8,128)(2,1)})) %all-reduce.15.cloned.1.call-update) | async-done | bytes 2359312 | tf_op jit(solution)/shard_map/psum | solution.py:102
  496.2 3.5 collective-permute-start.8
  502.0 4.6 collective-permute-start.9
  509.9 7.3 %collective-permute-start.10 = (bf16[72,256]{1,0:T(8,128)(2,1)S(1)}, bf16[72,256]{1,0:T(8,128)(2,1)S(1)}, u32[]{:S(2)}, u32[]{:S(2)}) collective-permute-start(bf16[72,256]{1,0:T(8,128)(2,1)S(1)} %collective-permute-done.9), channel_id=1, source_target_pairs={{0,128},{32,160},{64,192},{96,224},{128,0},{160,32},{192,64},{224,... | collective-permute-start | bytes 110600 | tf_op jit(solution)/shard_map/ppermute | solution.py:15
  (178 shorter events, 84.0 us)
Async XLA Ops:
  7.2 9.8 %copy-start = (bf16[1,1,16,16,256]{4,3,2,1,0:T(8,128)(2,1)S(1)}, bf16[1,1,16,16,256]{4,3,2,1,0:T(8,128)(2,1)}, u32[]{:S(2)}) copy-start(bf16[1,1,16,16,256]{4,3,2,1,0:T(8,128)(2,1)} %param.9) | copy-start | bytes 393220
  7.2 91.8 %all-gather.3.cloned.1.call-start = ((), (), s32[]{:S(2)}) async-start(), calls=%async_computation | async-start | bytes 1216512 | tf_op jit(solution)/shard_map/all_gather | solution.py:75
  8.8 174.3 %all-gather.5.cloned.1.call-start = ((), (), s32[]{:S(2)}) async-start(), calls=%async_computation.1 | async-start | bytes 1216512 | tf_op jit(solution)/shard_map/all_gather | solution.py:76
  8.8 23.9 %collective-permute-start.2 = (bf16[72,256]{1,0:T(8,128)(2,1)}, bf16[72,256]{1,0:T(8,128)(2,1)S(1)}, u32[]{:S(2)}, u32[]{:S(2)}) collective-permute-start(bf16[72,256]{1,0:T(8,128)(2,1)} %bitcast_convert_fusion), channel_id=1, source_target_pairs={{0,32},{32,0},{64,96},{96,64},{128,160},{160,128},{192,224},{224,1... | collective-permute-start | bytes 110600 | tf_op jit(solution)/shard_map/ppermute | solution.py:15
  32.7 17.9 %copy-start.17 = (bf16[1,16,16,2304]{3,2,1,0:T(8,128)(2,1)}, bf16[1,16,16,2304]{3,2,1,0:T(8,128)(2,1)S(1)}, u32[]{:S(2)}) copy-start(bf16[1,16,16,2304]{3,2,1,0:T(8,128)(2,1)S(1)} %constant_dynamic-update-slice_fusion.72) | copy-start | bytes 3538948
  32.8 8.0 %collective-permute-start.3 = (bf16[72,256]{1,0:T(8,128)(2,1)S(1)}, bf16[72,256]{1,0:T(8,128)(2,1)S(1)}, u32[]{:S(2)}, u32[]{:S(2)}) collective-permute-start(bf16[72,256]{1,0:T(8,128)(2,1)S(1)} %collective-permute-done.2), channel_id=1, source_target_pairs={{0,64},{32,96},{64,0},{96,32},{128,192},{160,224},{192,128},{224,1... | collective-permute-start | bytes 110600 | tf_op jit(solution)/shard_map/ppermute | solution.py:15
  40.8 11.1 %collective-permute-start.4 = (bf16[72,256]{1,0:T(8,128)(2,1)S(1)}, bf16[72,256]{1,0:T(8,128)(2,1)S(1)}, u32[]{:S(2)}, u32[]{:S(2)}) collective-permute-start(bf16[72,256]{1,0:T(8,128)(2,1)S(1)} %collective-permute-done.3), channel_id=1, source_target_pairs={{0,128},{32,160},{64,192},{96,224},{128,0},{160,32},{192,64},{224,... | collective-permute-start | bytes 110600 | tf_op jit(solution)/shard_map/ppermute | solution.py:15
  51.9 7.0 %collective-permute-start.5 = (bf16[72,256]{1,0:T(8,128)(2,1)S(1)}, bf16[72,256]{1,0:T(8,128)(2,1)S(1)}, u32[]{:S(2)}, u32[]{:S(2)}) collective-permute-start(bf16[72,256]{1,0:T(8,128)(2,1)S(1)} %collective-permute-done.4), channel_id=1, source_target_pairs={{0,256},{32,288},{64,320},{96,352},{128,384},{160,416},{192,448},{... | collective-permute-start | bytes 110600 | tf_op jit(solution)/shard_map/ppermute | solution.py:15
  59.5 435.9 %all-reduce.15.cloned.1.call-start = ((), (), s32[]{:S(2)}) async-start(), calls=%async_computation.2 | async-start | bytes 4718592 | tf_op jit(solution)/shard_map/psum | solution.py:102
  101.8 11.7 %collective-permute-start = (bf16[1,16,16,256]{3,2,1,0:T(8,128)(2,1)S(1)}, bf16[1,16,16,256]{3,2,1,0:T(8,128)(2,1)S(1)}, u32[]{:S(2)}, u32[]{:S(2)}) collective-permute-start(bf16[1,16,16,256]{3,2,1,0:T(8,128)(2,1)S(1)} %bitcast.548), channel_id=1, source_target_pairs={{32,0},{64,32},{96,64},{128,96},{160,128},{192,160},{224,192},{256... | collective-permute-start | bytes 393224 | tf_op jit(solution)/shard_map/ppermute | solution.py:21
  126.9 62.9 %collective-permute-start.1 = (bf16[1,16,16,256]{3,2,1,0:T(8,128)(2,1)}, bf16[1,16,16,256]{3,2,1,0:T(8,128)(2,1)S(1)}, u32[]{:S(2)}, u32[]{:S(2)}) collective-permute-start(bf16[1,16,16,256]{3,2,1,0:T(8,128)(2,1)} %fusion.125), channel_id=1, source_target_pairs={{32,0},{64,32},{96,64},{128,96},{160,128},{192,160},{224,192},{256... | collective-permute-start | bytes 393224 | tf_op jit(solution)/shard_map/ppermute | solution.py:21
  183.1 6.8 %copy-start.18 = (bf16[1,16,16,2304]{3,2,1,0:T(8,128)(2,1)S(1)}, bf16[1,16,16,2304]{3,2,1,0:T(8,128)(2,1)}, u32[]{:S(2)}) copy-start(bf16[1,16,16,2304]{3,2,1,0:T(8,128)(2,1)} %copy-done.17) | copy-start | bytes 3538948
  186.1 10.6 %collective-permute-start.6 = (bf16[1,16,16,256]{3,2,1,0:T(8,128)(2,1)S(1)}, bf16[1,16,16,256]{3,2,1,0:T(8,128)(2,1)S(1)}, u32[]{:S(2)}, u32[]{:S(2)}) collective-permute-start(bf16[1,16,16,256]{3,2,1,0:T(8,128)(2,1)S(1)} %bitcast.546), channel_id=1, source_target_pairs={{0,32},{32,64},{64,96},{96,128},{128,160},{160,192},{192,224},{224... | collective-permute-start | bytes 393224 | tf_op jit(solution)/shard_map/ppermute | solution.py:21
  209.6 5.8 %copy-start.8 = (bf16[1,16,16,256]{3,2,1,0:T(8,128)(2,1)}, bf16[1,16,16,256]{3,2,1,0:T(8,128)(2,1)S(1)}, u32[]{:S(2)}) copy-start(bf16[1,16,16,256]{3,2,1,0:T(8,128)(2,1)S(1)} %fusion.145) | copy-start | bytes 393220
  209.6 9.2 %copy-start.16 = (bf16[1,16,16,2304]{3,2,1,0:T(8,128)(2,1)S(1)}, bf16[1,16,16,2304]{3,2,1,0:T(8,128)(2,1)}, u32[]{:S(2)}) copy-start(bf16[1,16,16,2304]{3,2,1,0:T(8,128)(2,1)} %copy-done.15) | copy-start | bytes 3538948
  209.6 9.2 %collective-permute-start.7 = (bf16[1,16,16,256]{3,2,1,0:T(8,128)(2,1)S(1)}, bf16[1,16,16,256]{3,2,1,0:T(8,128)(2,1)S(1)}, u32[]{:S(2)}, u32[]{:S(2)}) collective-permute-start(bf16[1,16,16,256]{3,2,1,0:T(8,128)(2,1)S(1)} %fusion.145), channel_id=1, source_target_pairs={{0,32},{32,64},{64,96},{96,128},{128,160},{160,192},{192,224},{224... | collective-permute-start | bytes 393224 | tf_op jit(solution)/shard_map/ppermute | solution.py:21
  496.2 5.8 %collective-permute-start.8 = (bf16[72,256]{1,0:T(8,128)(2,1)S(1)}, bf16[72,256]{1,0:T(8,128)(2,1)S(1)}, u32[]{:S(2)}, u32[]{:S(2)}) collective-permute-start(bf16[72,256]{1,0:T(8,128)(2,1)S(1)} %convert_convert_fusion), channel_id=1, source_target_pairs={{0,32},{32,0},{64,96},{96,64},{128,160},{160,128},{192,224},{224,1... | collective-permute-start | bytes 110600 | tf_op jit(solution)/shard_map/ppermute | solution.py:15
  502.0 7.8 %collective-permute-start.9 = (bf16[72,256]{1,0:T(8,128)(2,1)S(1)}, bf16[72,256]{1,0:T(8,128)(2,1)S(1)}, u32[]{:S(2)}, u32[]{:S(2)}) collective-permute-start(bf16[72,256]{1,0:T(8,128)(2,1)S(1)} %collective-permute-done.8), channel_id=1, source_target_pairs={{0,64},{32,96},{64,0},{96,32},{128,192},{160,224},{192,128},{224,1... | collective-permute-start | bytes 110600 | tf_op jit(solution)/shard_map/ppermute | solution.py:15
  509.8 12.6 %copy-start.9 = (bf16[1,16,16,256]{3,2,1,0:T(8,128)(2,1)S(1)}, bf16[1,16,16,256]{3,2,1,0:T(8,128)(2,1)}, u32[]{:S(2)}) copy-start(bf16[1,16,16,256]{3,2,1,0:T(8,128)(2,1)} %copy-done.8) | copy-start | bytes 393220
  509.8 16.2 %copy-start.7 = (f32[1,72,256]{2,1,0:T(8,128)S(1)}, f32[1,72,256]{2,1,0:T(8,128)}, u32[]{:S(2)}) copy-start(f32[1,72,256]{2,1,0:T(8,128)} %param.11) | copy-start | bytes 221188
  509.9 16.2 %copy-start.10 = (f32[1,72,256]{2,1,0:T(8,128)S(1)}, f32[1,72,256]{2,1,0:T(8,128)}, u32[]{:S(2)}) copy-start(f32[1,72,256]{2,1,0:T(8,128)} %param.13) | copy-start | bytes 221188
  509.9 16.2 %copy-start.11 = (f32[1,72,256]{2,1,0:T(8,128)S(1)}, f32[1,72,256]{2,1,0:T(8,128)}, u32[]{:S(2)}) copy-start(f32[1,72,256]{2,1,0:T(8,128)} %param.12) | copy-start | bytes 221188
  509.9 10.3 %collective-permute-start.10 = (bf16[72,256]{1,0:T(8,128)(2,1)S(1)}, bf16[72,256]{1,0:T(8,128)(2,1)S(1)}, u32[]{:S(2)}, u32[]{:S(2)}) collective-permute-start(bf16[72,256]{1,0:T(8,128)(2,1)S(1)} %collective-permute-done.9), channel_id=1, source_target_pairs={{0,128},{32,160},{64,192},{96,224},{128,0},{160,32},{192,64},{224,... | collective-permute-start | bytes 110600 | tf_op jit(solution)/shard_map/ppermute | solution.py:15
  520.2 5.8 %collective-permute-start.11 = (bf16[72,256]{1,0:T(8,128)(2,1)S(1)}, bf16[72,256]{1,0:T(8,128)(2,1)S(1)}, u32[]{:S(2)}, u32[]{:S(2)}) collective-permute-start(bf16[72,256]{1,0:T(8,128)(2,1)S(1)} %collective-permute-done.10), channel_id=1, source_target_pairs={{0,256},{32,288},{64,320},{96,352},{128,384},{160,416},{192,448},{... | collective-permute-start | bytes 110600 | tf_op jit(solution)/shard_map/ppermute | solution.py:15
  (10 other events, 23.1 us)
Sparse Core Ops, SparseCore 0:
  11.8 87.0 all-gather.2
  102.8 80.2 all-gather.4
  221.1 274.2 all-reduce.14
where the time goes:
time: 535 us; the launch traced here: 534 us
  waiting for transfers between devices  360 us (67%)
  local copies, waits for them, and re-layouts  65.3 us (12%)
  starting transfers between devices  57.3 us (11%)
  matrix products  28.5 us (5%)
  between operations  14.5 us (3%)
  other arithmetic  8.8 us (2%)
    psum x1, waiting for transfers between devices, per_device(): lax.psum(term_up.astype(jnp.bfloat16), 'dp').astype(jnp.float32)  257 us
    all_gather x1, waiting for transfers between devices, per_device(): lax.all_gather(mirror_rows, 'dp', axis=0, tiled=True)  51.5 us
    unnamed x126, local copies, waits for them, and re-layouts  40.9 us
    ppermute x8, starting transfers between devices, from_partner(): lax.ppermute(value, axis, [(i, i ^ 1 << stride) for i in range(lax.axis_s...  40 us
    all_gather x1, waiting for transfers between devices, per_device(): lax.all_gather(own_rows, 'dp', axis=0, tiled=True)  35.4 us
    dot_general x6, local copies, waits for them, and re-layouts, section_front(): lax.dot_general(taps_front, kernel, (((1, 2), (0, 2)), ((), ())), preferr...  19.1 us
    ppermute x4, starting transfers between devices, passed_along(): return lax.ppermute(value, axis, pairs)  17.2 us
    dot_general x6, matrix products, section_front(): lax.dot_general(taps_front, kernel, (((1, 2), (0, 2)), ((), ())), preferr...  16.9 us
  transfers between devices with their start and end apart: 15, of which 10 were waited for; matrix products, arithmetic and copies ran while one was open for 15% of the time, Pallas kernels for 0%

commit v1 on v0

--- a/solution.py
+++ b/solution.py
@@ -9,6 +9,12 @@
 learn_rate = 0.01
 decay_rate = 0.1
 epsilon = 1e-08
+
+
+def solve_points_over_axis(chunk):
+    r2 = lax.all_gather(chunk, "dp")
+    opened = jnp.sum(r2, axis=0)
+    return opened
 
 
 def from_partner(value, axis, stride):
@@ -99,7 +105,7 @@
     term_up = weight_term(hidden_up, seen_up)
     full_down, full_up = (
         lax.psum(term_down.astype(jnp.bfloat16), "dp").astype(jnp.float32),
-        lax.psum(term_up.astype(jnp.bfloat16), "dp").astype(jnp.float32),
+        solve_points_over_axis(term_up.astype(jnp.bfloat16)).astype(jnp.float32),
     )
     shard_rows = term_down.shape[0] // lax.axis_size("dp")
     row_start = lax.axis_index("dp") * shard_rows

time: 535 us -> 748 us (1.40)
  the two profiles are of different devices: /device:TPU:2 before, /device:TPU:4 now
where the time goes in v1:
time: 748 us; the launch traced here: 747 us
  waiting for transfers between devices  582 us (78%)
  starting transfers between devices  54.1 us (7%)
  local copies, waits for them, and re-layouts  51.8 us (7%)
  matrix products  25.1 us (3%)
  other arithmetic  19.4 us (3%)
  between operations  14.6 us (2%)
    psum x1, waiting for transfers between devices, per_device(): lax.psum(term_down.astype(jnp.bfloat16), 'dp').astype(jnp.float32)  234 us
    all_gather x1, waiting for transfers between devices, solve_points_over_axis(): r2 = lax.all_gather(chunk, 'dp')  206 us
    all_gather x1, waiting for transfers between devices, per_device(): lax.all_gather(mirror_rows, 'dp', axis=0, tiled=True)  73.2 us
    ppermute x8, starting transfers between devices, from_partner(): lax.ppermute(value, axis, [(i, i ^ 1 << stride) for i in range(lax.axis_s...  43.3 us
    all_gather x1, waiting for transfers between devices, per_device(): lax.all_gather(own_rows, 'dp', axis=0, tiled=True)  43.2 us
    unnamed x122, local copies, waits for them, and re-layouts  31.6 us
    dot_general x6, matrix products, section_front(): lax.dot_general(taps_front, kernel, (((1, 2), (0, 2)), ((), ())), preferr...  17 us
  transfers between devices with their start and end apart: 16, of which 14 were waited for; matrix products, arithmetic and copies ran while one was open for 12% of the time, Pallas kernels for 0%

profile of v1, /device:TPU:4, one launch (start us, length us, event | category | flops | bytes accessed | tf_op | source)
XLA Modules:
  0.0 747.2 jit_solution(17761983690800165120)
XLA Ops:
  8.1 4.3 collective-permute-start.2
  14.3 6.1 collective-permute-start.3
  22.4 9.3 %collective-permute-start.4 = (bf16[72,256]{1,0:T(8,128)(2,1)S(1)}, bf16[72,256]{1,0:T(8,128)(2,1)S(1)}, u32[]{:S(2)}, u32[]{:S(2)}) collective-permute-start(bf16[72,256]{1,0:T(8,128)(2,1)S(1)} %collective-permute-done.3), channel_id=1, source_target_pairs={{0,128},{32,160},{64,192},{96,224},{128,0},{160,32},{192,64},{224,... | collective-permute-start | bytes 110600 | tf_op jit(solution)/shard_map/ppermute | solution.py:21
  33.6 3.1 collective-permute-start.5
  50.1 73.2 %all-gather.7.cloned.1.call-done = bf16[2304,256]{1,0:T(8,128)(2,1)} async-done(((bf16[72,256]{1,0:T(8,128)(2,1)}), bf16[2304,256]{1,0:T(8,128)(2,1)}) %all-gather.7.cloned.1.call-update) | async-done | bytes 1179664 | tf_op jit(solution)/shard_map/all_gather | solution.py:82
  123.3 2.9 fusion.139
  126.1 3.6 collective-permute-start.6
  139.1 3.6 dot_general.56
  142.6 3.0 fusion.145
  145.7 4.4 collective-permute-start.7
  164.2 43.2 %all-gather.5.cloned.1.call-done = bf16[2304,256]{1,0:T(8,128)(2,1)} async-done(((bf16[72,256]{1,0:T(8,128)(2,1)}), bf16[2304,256]{1,0:T(8,128)(2,1)}) %all-gather.5.cloned.1.call-update) | async-done | bytes 1179664 | tf_op jit(solution)/shard_map/all_gather | solution.py:81
  213.1 4.7 collective-permute-done
  224.0 3.7 dot_general.50
  227.7 3.6 fusion.125
  233.9 4.4 collective-permute-done.1
  244.6 3.6 dot_general.52
  249.9 2.9 fusion.7
  258.7 205.6 %all-gather.9.cloned.1.call-done = bf16[73728,256]{1,0:T(8,128)(2,1)} async-done(((bf16[2304,256]{1,0:T(8,128)(2,1)}), bf16[73728,256]{1,0:T(8,128)(2,1)}) %all-gather.9.cloned.1.call-update) | async-done | bytes 37748752 | tf_op jit(solution)/shard_map/all_gather | solution.py:15
  464.2 12.7 %reduce_sum.12 = bf16[2304,256]{1,0:T(8,128)(2,1)S(1)} reduce(bf16[32,2304,256]{2,1,0:T(8,128)(2,1)} %bitcast.513, bf16[]{:T(256)} %constant.18.clone.1), dimensions={0}, to_apply=%region_1.2 | reduce | flops 18284544 | bytes 38928384 | tf_op jit(solution)/shard_map/reduce_sum | solution.py:16
  476.9 3.6 collective-permute-start.8
  482.9 4.6 collective-permute-start.9
  489.9 8.4 %collective-permute-start.10 = (bf16[72,256]{1,0:T(8,128)(2,1)}, bf16[72,256]{1,0:T(8,128)(2,1)S(1)}, u32[]{:S(2)}, u32[]{:S(2)}) collective-permute-start(bf16[72,256]{1,0:T(8,128)(2,1)} %collective-permute-done.9), channel_id=1, source_target_pairs={{0,128},{32,160},{64,192},{96,224},{128,0},{160,32},{192,64},{224,... | collective-permute-start | bytes 110600 | tf_op jit(solution)/shard_map/ppermute | solution.py:21
  500.6 4.0 collective-permute-start.11
  505.3 233.8 %all-reduce.14.cloned.1.call-done = bf16[2304,256]{1,0:T(8,128)(2,1)} async-done(((bf16[2304,256]{1,0:T(8,128)(2,1)}), bf16[2304,256]{1,0:T(8,128)(2,1)}) %all-reduce.14.cloned.1.call-update) | async-done | bytes 1179664 | tf_op jit(solution)/shard_map/psum | solution.py:107
  (178 shorter events, 80.8 us)
Async XLA Ops:
  7.2 37.5 %copy-start = (bf16[1,1,16,16,256]{4,3,2,1,0:T(8,128)(2,1)S(1)}, bf16[1,1,16,16,256]{4,3,2,1,0:T(8,128)(2,1)}, u32[]{:S(2)}) copy-start(bf16[1,1,16,16,256]{4,3,2,1,0:T(8,128)(2,1)} %param.10) | copy-start | bytes 393220
  7.2 116.1 %all-gather.7.cloned.1.call-start = ((), (), s32[]{:S(2)}) async-start(), calls=%async_computation.1 | async-start | bytes 1216512 | tf_op jit(solution)/shard_map/all_gather | solution.py:82
  8.1 32.0 %copy-start.5 = (bf16[72,256]{1,0:T(8,128)(2,1)}, bf16[72,256]{1,0:T(8,128)(2,1)S(1)}, u32[]{:S(2)}) copy-start(bf16[72,256]{1,0:T(8,128)(2,1)S(1)} %bitcast_convert_fusion) | copy-start | bytes 110596
  8.1 6.2 collective-permute-start.2
  14.3 8.0 %collective-permute-start.3 = (bf16[72,256]{1,0:T(8,128)(2,1)S(1)}, bf16[72,256]{1,0:T(8,128)(2,1)S(1)}, u32[]{:S(2)}, u32[]{:S(2)}) collective-permute-start(bf16[72,256]{1,0:T(8,128)(2,1)S(1)} %collective-permute-done.2), channel_id=1, source_target_pairs={{0,64},{32,96},{64,0},{96,32},{128,192},{160,224},{192,128},{224,1... | collective-permute-start | bytes 110600 | tf_op jit(solution)/shard_map/ppermute | solution.py:21
  22.4 11.2 %collective-permute-start.4 = (bf16[72,256]{1,0:T(8,128)(2,1)S(1)}, bf16[72,256]{1,0:T(8,128)(2,1)S(1)}, u32[]{:S(2)}, u32[]{:S(2)}) collective-permute-start(bf16[72,256]{1,0:T(8,128)(2,1)S(1)} %collective-permute-done.3), channel_id=1, source_target_pairs={{0,128},{32,160},{64,192},{96,224},{128,0},{160,32},{192,64},{224,... | collective-permute-start | bytes 110600 | tf_op jit(solution)/shard_map/ppermute | solution.py:21
  33.6 5.8 collective-permute-start.5
  40.1 167.4 %all-gather.5.cloned.1.call-start = ((), (), s32[]{:S(2)}) async-start(), calls=%async_computation | async-start | bytes 1216512 | tf_op jit(solution)/shard_map/all_gather | solution.py:81
  40.8 423.4 %all-gather.9.cloned.1.call-start = ((), (), s32[]{:S(2)}) async-start(), calls=%async_computation.3 | async-start | bytes 38928384 | tf_op jit(solution)/shard_map/all_gather | solution.py:15
  126.1 6.7 collective-permute-start.6
  142.6 9.9 %copy-start.14 = (bf16[1,16,16,2304]{3,2,1,0:T(8,128)(2,1)S(1)}, bf16[1,16,16,2304]{3,2,1,0:T(8,128)(2,1)}, u32[]{:S(2)}) copy-start(bf16[1,16,16,2304]{3,2,1,0:T(8,128)(2,1)} %constant_dynamic-update-slice_fusion.99) | copy-start | bytes 3538948
  145.7 7.4 copy-start.6
  145.7 6.9 collective-permute-start.7
  154.8 584.3 %all-reduce.14.cloned.1.call-start = ((), (), s32[]{:S(2)}) async-start(), calls=%async_computation.2 | async-start | bytes 2359296 | tf_op jit(solution)/shard_map/psum | solution.py:107
  210.3 7.5 %collective-permute-start = (bf16[1,16,16,256]{3,2,1,0:T(8,128)(2,1)S(1)}, bf16[1,16,16,256]{3,2,1,0:T(8,128)(2,1)S(1)}, u32[]{:S(2)}, u32[]{:S(2)}) collective-permute-start(bf16[1,16,16,256]{3,2,1,0:T(8,128)(2,1)S(1)} %bitcast.551), channel_id=1, source_target_pairs={{32,0},{64,32},{96,64},{128,96},{160,128},{192,160},{224,192},{256... | collective-permute-start | bytes 393224 | tf_op jit(solution)/shard_map/ppermute | solution.py:27
  231.2 7.1 collective-permute-start.1
  476.9 6.0 collective-permute-start.8
  482.9 7.1 collective-permute-start.9
  488.2 16.3 %copy-start.7 = (bf16[1,16,16,256]{3,2,1,0:T(8,128)(2,1)S(1)}, bf16[1,16,16,256]{3,2,1,0:T(8,128)(2,1)}, u32[]{:S(2)}) copy-start(bf16[1,16,16,256]{3,2,1,0:T(8,128)(2,1)} %copy-done.6) | copy-start | bytes 393220
  488.2 250.9 %copy-start.4 = (f32[1,72,256]{2,1,0:T(8,128)S(1)}, f32[1,72,256]{2,1,0:T(8,128)}, u32[]{:S(2)}) copy-start(f32[1,72,256]{2,1,0:T(8,128)} %param.11) | copy-start | bytes 221188
  488.3 250.9 %copy-start.8 = (f32[1,72,256]{2,1,0:T(8,128)S(1)}, f32[1,72,256]{2,1,0:T(8,128)}, u32[]{:S(2)}) copy-start(f32[1,72,256]{2,1,0:T(8,128)} %param.13) | copy-start | bytes 221188
  488.3 250.9 %copy-start.9 = (f32[1,72,256]{2,1,0:T(8,128)S(1)}, f32[1,72,256]{2,1,0:T(8,128)}, u32[]{:S(2)}) copy-start(f32[1,72,256]{2,1,0:T(8,128)} %param.12) | copy-start | bytes 221188
  489.9 10.6 %collective-permute-start.10 = (bf16[72,256]{1,0:T(8,128)(2,1)}, bf16[72,256]{1,0:T(8,128)(2,1)S(1)}, u32[]{:S(2)}, u32[]{:S(2)}) collective-permute-start(bf16[72,256]{1,0:T(8,128)(2,1)} %collective-permute-done.9), channel_id=1, source_target_pairs={{0,128},{32,160},{64,192},{96,224},{128,0},{160,32},{192,64},{224,... | collective-permute-start | bytes 110600 | tf_op jit(solution)/shard_map/ppermute | solution.py:21
  500.6 238.6 %collective-permute-start.11 = (bf16[72,256]{1,0:T(8,128)(2,1)S(1)}, bf16[72,256]{1,0:T(8,128)(2,1)S(1)}, u32[]{:S(2)}, u32[]{:S(2)}) collective-permute-start(bf16[72,256]{1,0:T(8,128)(2,1)S(1)} %collective-permute-done.10), channel_id=1, source_target_pairs={{0,256},{32,288},{64,320},{96,352},{128,384},{160,416},{192,448},{... | collective-permute-start | bytes 110600 | tf_op jit(solution)/shard_map/ppermute | solution.py:21
  (9 other events, 17.5 us)
Sparse Core Ops, SparseCore 0:
  40.2 83.0 all-gather.6
  127.1 80.2 all-gather.4
  210.8 253.3 all-gather.8
  467.0 272.1 all-reduce.13
